TPU v7x, 32 devices: a whole 2x2x4 slice. The times are simulated.
32 devices in a mesh: grp: 2 (over y), tr: 8 (over z, x), root: 2 (over core).
Axes of the slice: x: 2, y: 2, z: 4, core: 2. Of those that a mesh axis runs over, the one named last changes fastest.
Arguments:
- residual: bfloat16 [128, 65536], P('root', ('grp', 'tr')), parts along dimension 1, may hold values from -8 to 8
- subspace: bfloat16 [512, 65536], P(None, ('grp', 'tr')), parts along dimension 1, may hold values from -1 to 1, as said below
- inverses: bfloat16 [16, 512, 512], P(('grp', 'tr')), parts along dimension 0, may hold values from -1 to 3, as said below
- owner_offset: int32 [128], P(('grp', 'tr')), parts along dimension 0, may hold values from 0 to 3, as said below
- listed: int32 [128], P(('grp', 'tr')), parts along dimension 0, may hold values from 0 to 1, as said below
Outputs:
- corrections: float32 [128, 65536], P('root', ('grp', 'tr')), parts along dimension 1
There are 2 independent parts, one for each index of `grp`. A program takes and returns all parts, laid end to end along the dimension named above; each array names one. Nothing has to cross between parts.
Inputs may be any that keep to these rules, and one draw needn't show every extreme that they name: Each entry of subspace lies within the stated range; rows are not normalized. `inverses`: each inverse is a dense real matrix. `owner_offset`: among the 8 blocks of each shard, at least one is listed and has offset 3. Each shard has at least one listed block and at least one unlisted block.
All inputs are finite; a program needn't handle non-finite values.
Results may differ from a plain program's by a relative error of at most 0.0065.
Values may be sent and summed in bfloat16 or wider, within the bound.
A program may use at most 64 MiB of HBM per device.

v0:
```python
import jax
import jax.numpy as jnp
from jax import lax
from jax.sharding import PartitionSpec as P

BLK = 512
OFFS = 4
PASSES = 2


def from_behind(block, axis, distance):
    devices = range(lax.axis_size(axis))
    route = [((i - distance) % len(devices), i) for i in devices]
    return lax.ppermute(block, axis, route)


def per_device(residual, subspace, inverses, owner_offset, listed):
    root_count, row_count = residual.shape
    block_count = row_count // BLK
    blocks = residual.reshape(root_count, block_count, BLK)
    chosen_mask = listed > 0
    inverse = inverses[0]
    target = jnp.arange(OFFS, dtype=jnp.int32)
    held_inverses = [inverse]
    for offset in range(1, OFFS):
        held_inverses.append(from_behind(inverse, "tr", -offset))
    inverse_table = jnp.stack(held_inverses)
    selector = (owner_offset[:, None] == target[None, :]).astype(jnp.bfloat16)
    picked = jnp.einsum(
        "jd,dbc->jbc", selector, inverse_table, preferred_element_type=jnp.float32
    ).astype(jnp.bfloat16)
    solved = jnp.einsum("rjb,jbc->rjc", blocks, picked, preferred_element_type=jnp.float32)
    precond = jnp.where(chosen_mask[None, :, None], solved, blocks.astype(jnp.float32)).reshape(
        root_count, row_count
    )
    current = precond
    for repeat in range(PASSES):
        rounded = current.astype(jnp.bfloat16)
        partial_correlation = lax.dot_general(
            rounded, subspace, (((1,), (1,)), ((), ())), preferred_element_type=jnp.float32
        )
        correlation = lax.psum(partial_correlation, "tr")
        coefficients = correlation.astype(jnp.bfloat16)
        current = current - jnp.dot(coefficients, subspace, preferred_element_type=jnp.float32)
    return current


def solution(mesh):
    return jax.shard_map(
        per_device,
        mesh=mesh,
        in_specs=(
            P("root", ("grp", "tr")),
            P(None, ("grp", "tr")),
            P(("grp", "tr"), None, None),
            P(("grp", "tr")),
            P(("grp", "tr")),
        ),
        out_specs=P("root", ("grp", "tr")),
        check_vma=False,
    )
```

profile of v0, /device:TPU:0, one launch (start us, length us, event | category | flops | bytes accessed | tf_op | source)
XLA Modules:
  0.0 140.2 jit_solution(10332493646921314701)
XLA Ops:
  0.0 0.0 copy-start.2
  0.0 6.0 %collective-permute-start = (bf16[512,512]{1,0:T(8,128)(2,1)}, bf16[512,512]{1,0:T(8,128)(2,1)S(1)}, u32[]{:S(2)}, u32[]{:S(2)}) collective-permute-start(bf16[512,512]{1,0:T(8,128)(2,1)} %bitcast.28), channel_id=1, source_target_pairs={{2,0},{4,2},{6,4},{8,6},{10,8},{12,10},{14,12},{0,14},{3,1},{5,3},... | collective-permute-start | bytes 1572872 | tf_op jit(solution)/shard_map/ppermute | solution.py:14
  6.0 0.4 collective-permute-start.1
  6.5 0.0 collective-permute-start.2
  6.5 0.7 broadcast_compare_fusion
  7.1 11.6 %collective-permute-done = bf16[512,512]{1,0:T(8,128)(2,1)S(1)} collective-permute-done((bf16[512,512]{1,0:T(8,128)(2,1)}, bf16[512,512]{1,0:T(8,128)(2,1)S(1)}, u32[]{:S(2)}, u32[]{:S(2)}) %collective-permute-start) | collective-permute-done | bytes 524320 | tf_op jit(solution)/shard_map/ppermute | solution.py:14
  18.7 11.2 %collective-permute-done.1 = bf16[512,512]{1,0:T(8,128)(2,1)S(1)} collective-permute-done((bf16[512,512]{1,0:T(8,128)(2,1)}, bf16[512,512]{1,0:T(8,128)(2,1)S(1)}, u32[]{:S(2)}, u32[]{:S(2)}) %collective-permute-start.1) | collective-permute-done | bytes 524320 | tf_op jit(solution)/shard_map/ppermute | solution.py:14
  29.9 10.1 %collective-permute-done.2 = bf16[512,512]{1,0:T(8,128)(2,1)S(1)} collective-permute-done((bf16[512,512]{1,0:T(8,128)(2,1)}, bf16[512,512]{1,0:T(8,128)(2,1)S(1)}, u32[]{:S(2)}, u32[]{:S(2)}) %collective-permute-start.2) | collective-permute-done | bytes 524320 | tf_op jit(solution)/shard_map/ppermute | solution.py:14
  40.0 1.3 pad_maximum_fusion
  41.3 0.0 copy-done.2
  41.3 0.0 copy-start.3
  41.3 1.5 %fusion.1 = bf16[8,512,512]{2,0,1:T(8,128)(2,1)S(1)} fusion(bf16[4,512,512]{2,1,0:T(8,128)(2,1)S(1)} %pad_maximum_fusion, s32[8]{0:T(128)S(1)} %copy-done.2), kind=kOutput, calls=%fused_computation.5 | convolution fusion | flops 16777248 | bytes 6291488 | tf_op jit(solution)/shard_map/jd,dbc->jbc/dot_general | solution.py:29
  42.9 0.0 copy-done.3
  42.9 0.0 copy-start
  42.9 2.5 %fusion.5 = f32[8,8,8,512]{3,2,1,0:T(8,128)S(1)} fusion(bf16[8,512,512]{2,0,1:T(8,128)(2,1)S(1)} %fusion.1, bf16[8,8,8,512]{3,2,1,0:T(8,128)(2,1)S(1)} %bitcast.34, pred[8]{0:T(512)(128)(4,1)S(1)} %broadcast_compare_fusion), kind=kOutput, calls=%fused_computation.9 | convolution fusion | flops 268959744 | bytes 5767176 | tf_op jit(solution)/shard_map/rjb,jbc->rjc/dot_general | solution.py:32
  45.4 0.1 copy.12
  45.4 0.0 copy-done
  45.5 1.4 %fusion.10 = f32[64,512]{1,0:T(8,128)S(1)} fusion(bf16[512,4096]{1,0:T(8,128)(2,1)S(1)} %copy-done, f32[64,4096]{1,0:T(8,128)S(1)} %bitcast.26), kind=kOutput, calls=%fused_computation.14 | convolution fusion | flops 268697600 | bytes 5373952 | tf_op jit(solution)/shard_map/dot_general | solution.py:39
  46.9 50.4 %all-reduce.2 = bf16[64,512]{1,0:T(8,128)(2,1)S(1)} all-reduce(f32[64,512]{1,0:T(8,128)S(1)} %fusion.10), channel_id=1, replica_groups=mesh['grp'=2,'tr'=8,'root'=2] {'tr'}, use_global_device_ids=true, to_apply=%region_0.1 | all-reduce | flops 32768 | bytes 196608 | tf_op jit(solution)/shard_map/psum | solution.py:42
  97.2 0.0 copy-start.1
  97.2 3.2 %convolution_subtract_fusion.1 = f32[64,4096]{1,0:T(8,128)S(1)} fusion(f32[64,4096]{1,0:T(8,128)S(1)} %bitcast.27, bf16[512,4096]{1,0:T(8,128)(2,1)} %param.6, bf16[64,512]{1,0:T(8,128)(2,1)S(1)} %all-reduce.2), kind=kOutput, calls=%fused_computation.2 | convolution fusion | flops 268697600 | bytes 6356992 | tf_op jit(solution)/shard_map/dot_general | solution.py:44
  100.4 0.3 copy-done.1
  100.7 1.4 fusion.8
  102.1 34.1 %all-reduce.3 = bf16[64,512]{1,0:T(8,128)(2,1)S(1)} all-reduce(f32[64,512]{1,0:T(8,128)S(1)} %fusion.8), channel_id=1, replica_groups=mesh['grp'=2,'tr'=8,'root'=2] {'tr'}, use_global_device_ids=true, to_apply=%region_1.2 | all-reduce | flops 32768 | bytes 196608 | tf_op jit(solution)/shard_map/psum | solution.py:42
  136.2 4.0 %convolution_subtract_fusion = f32[64,4096]{1,0:T(8,128)} fusion(f32[64,4096]{1,0:T(8,128)S(1)} %convolution_subtract_fusion.1, bf16[512,4096]{1,0:T(8,128)(2,1)} %param.6, bf16[64,512]{1,0:T(8,128)(2,1)S(1)} %all-reduce.3), kind=kOutput, calls=%fused_computation.1 | convolution fusion | flops 268697600 | bytes 6356992 | tf_op jit(solution)/shard_map/dot_general | solution.py:44
Async XLA Ops:
  0.0 41.3 %copy-start.2 = (s32[8]{0:T(128)S(1)}, s32[8]{0:T(128)}, u32[]{:S(2)}) copy-start(s32[8]{0:T(128)} %param.8) | copy-start | bytes 100
  0.0 18.7 %collective-permute-start = (bf16[512,512]{1,0:T(8,128)(2,1)}, bf16[512,512]{1,0:T(8,128)(2,1)S(1)}, u32[]{:S(2)}, u32[]{:S(2)}) collective-permute-start(bf16[512,512]{1,0:T(8,128)(2,1)} %bitcast.28), channel_id=1, source_target_pairs={{2,0},{4,2},{6,4},{8,6},{10,8},{12,10},{14,12},{0,14},{3,1},{5,3},... | collective-permute-start | bytes 1572872 | tf_op jit(solution)/shard_map/ppermute | solution.py:14
  6.0 23.9 %collective-permute-start.1 = (bf16[512,512]{1,0:T(8,128)(2,1)}, bf16[512,512]{1,0:T(8,128)(2,1)S(1)}, u32[]{:S(2)}, u32[]{:S(2)}) collective-permute-start(bf16[512,512]{1,0:T(8,128)(2,1)} %bitcast.29), channel_id=1, source_target_pairs={{4,0},{6,2},{8,4},{10,6},{12,8},{14,10},{0,12},{2,14},{5,1},{7,3},... | collective-permute-start | bytes 1572872 | tf_op jit(solution)/shard_map/ppermute | solution.py:14
  6.5 33.6 %collective-permute-start.2 = (bf16[512,512]{1,0:T(8,128)(2,1)}, bf16[512,512]{1,0:T(8,128)(2,1)S(1)}, u32[]{:S(2)}, u32[]{:S(2)}) collective-permute-start(bf16[512,512]{1,0:T(8,128)(2,1)} %bitcast.30), channel_id=1, source_target_pairs={{6,0},{8,2},{10,4},{12,6},{14,8},{0,10},{2,12},{4,14},{7,1},{9,3},... | collective-permute-start | bytes 1572872 | tf_op jit(solution)/shard_map/ppermute | solution.py:14
  41.3 1.5 %copy-start.3 = (bf16[64,4096]{1,0:T(8,128)(2,1)S(1)}, bf16[64,4096]{1,0:T(8,128)(2,1)}, u32[]{:S(2)}) copy-start(bf16[64,4096]{1,0:T(8,128)(2,1)} %param.5) | copy-start | bytes 1572868
  42.9 2.6 %copy-start = (bf16[512,4096]{1,0:T(8,128)(2,1)S(1)}, bf16[512,4096]{1,0:T(8,128)(2,1)}, u32[]{:S(2)}) copy-start(bf16[512,4096]{1,0:T(8,128)(2,1)} %param.6) | copy-start | bytes 12582916
  97.2 3.5 %copy-start.1 = (bf16[512,4096]{1,0:T(8,128)(2,1)S(1)}, bf16[512,4096]{1,0:T(8,128)(2,1)}, u32[]{:S(2)}) copy-start(bf16[512,4096]{1,0:T(8,128)(2,1)} %param.6) | copy-start | bytes 12582916
where the time goes:
time: 140 us
  blocking collectives  84.5 us (60%)
  waiting for transfers between devices  32.9 us (24%)
  matrix products  14 us (10%)
  starting transfers between devices  6.46 us (5%)
  other arithmetic  1.96 us (1%)
    psum x2, blocking collectives, per_device(): correlation = lax.psum(partial_correlation, 'tr')  84.5 us
    ppermute x3, waiting for transfers between devices, from_behind(): return lax.ppermute(block, axis, route)  32.9 us
    dot_general x2, matrix products, per_device(): jnp.dot(coefficients, subspace, preferred_element_type=jnp.float32)  7.19 us
    ppermute x3, starting transfers between devices, from_behind(): return lax.ppermute(block, axis, route)  6.46 us
    dot_general x2, matrix products, per_device(): lax.dot_general(rounded, subspace, (((1,), (1,)), ((), ())), preferred_el...  2.8 us
  transfers between devices with their start and end apart: 3, of which 3 were waited for; matrix products, arithmetic and copies ran while one was open for 0% of the time, Pallas kernels for 0%

commit v1 on v0

v1 whole, which is shorter than its diff:
```python
import functools
import jax
import jax.numpy as jnp
from jax import lax
from jax.experimental import pallas as pl
from jax.experimental.pallas import tpu as pltpu
from jax.sharding import PartitionSpec as P

OFFS = 4
PASSES = 2
SUBLANES = 8
MESH = pl.DeviceIdType.MESH


def each(count, body):
    if count <= 16:
        for i in range(count):
            body(i)
    else:
        pl.loop(0, count)(body)


def kernel(n, roots, off, listed, res, sub, inv, out, table, res_v, sub_v, work, picked,
           partial, inbox, slabs, load_sem, part_send, part_recv, swap_send, swap_recv,
           rs_send, rs_recv, ag_send, ag_recv, out_sem):
    me = lax.axis_index("tr")
    root = lax.axis_index("root")
    rows, cols = res.shape
    blk = inv.shape[1]
    blocks = cols // blk
    spans = sub.shape[0]
    share = blk // roots
    owners = slabs.shape[1]
    slab = rows // owners
    mine = pl.ds(pl.multiple_of(root * share, share), share)

    def block(b):
        return pl.ds(b * blk, blk)

    own_load = pltpu.make_async_copy(inv.at[0], table.at[0], load_sem.at[0])
    own_load.start()
    res_load = pltpu.make_async_copy(res, res_v, load_sem.at[1])
    res_load.start()
    sub_load = pltpu.make_async_copy(sub, sub_v, load_sem.at[2])
    sub_load.start()

    barrier = pltpu.get_barrier_semaphore()

    def greet(d):
        pl.semaphore_signal(barrier, inc=1, device_id={"tr": lax.rem(me + d + 1, n)}, device_id_type=MESH)

    each(n - 1, greet)
    for d in range(1, roots):
        pl.semaphore_signal(barrier, inc=1, device_id={"root": lax.rem(root + d, roots)}, device_id_type=MESH)
    pl.semaphore_wait(barrier, n - 1 + roots - 1)

    def part_copy(o):
        return pltpu.make_async_remote_copy(
            src_ref=inv.at[0, mine], dst_ref=table.at[o, mine],
            send_sem=part_send.at[o], recv_sem=part_recv.at[o],
            device_id={"tr": lax.rem(me + n - o, n)}, device_id_type=MESH)

    def swap_copy(o, d):
        return pltpu.make_async_remote_copy(
            src_ref=table.at[o, mine], dst_ref=table.at[o, mine],
            send_sem=swap_send.at[o, d], recv_sem=swap_recv.at[o, d],
            device_id={"root": lax.rem(root + d, roots)}, device_id_type=MESH)

    def swap_in(o, d):
        other = lax.rem(root + roots - d, roots)
        theirs = pl.ds(pl.multiple_of(other * share, share), share)
        return pltpu.make_async_remote_copy(
            src_ref=table.at[o, theirs], dst_ref=table.at[o, theirs],
            send_sem=swap_send.at[o, d], recv_sem=swap_recv.at[o, d],
            device_id={"root": other}, device_id_type=MESH)

    for o in range(1, OFFS):
        part_copy(o).start()

    res_load.wait()
    for b in range(blocks):
        kept = jnp.where(listed[b] > 0, 0.0, res_v[:, block(b)].astype(jnp.float32))
        work[:, block(b)] = kept

    def apply(o):
        for b in range(blocks):
            hit = jnp.logical_and(listed[b] > 0, off[b] == o)
            x = res_v[:, block(b)].astype(jnp.float32)
            picked[pl.ds(b * rows, rows), :] = jnp.where(hit, x, 0.0).astype(jnp.bfloat16)
        for b in range(blocks):
            part = jnp.dot(picked[pl.ds(b * rows, rows), :], table[o], preferred_element_type=jnp.float32)
            work[:, block(b)] += part

    own_load.wait()
    apply(0)
    for o in range(1, OFFS):
        part_copy(o).wait_recv()
        for d in range(1, roots):
            swap_copy(o, d).start()
        for d in range(1, roots):
            swap_in(o, d).wait_recv()
        apply(o)
    sub_load.wait()

    def rows_of(j):
        return pl.ds(pl.multiple_of(j * slab, slab), slab)

    def rs_copy(k, d):
        peer = lax.rem(me + d + 1, n)
        return peer, pltpu.make_async_remote_copy(
            src_ref=partial.at[k, rows_of(lax.rem(peer, owners))], dst_ref=inbox.at[k, me],
            send_sem=rs_send.at[k, d], recv_sem=rs_recv.at[k, me],
            device_id={"tr": peer}, device_id_type=MESH)

    def rs_in(k, d):
        peer = lax.rem(me + d + 1, n)
        return peer, pltpu.make_async_remote_copy(
            src_ref=inbox.at[k, peer], dst_ref=inbox.at[k, peer],
            send_sem=rs_send.at[k, d], recv_sem=rs_recv.at[k, peer],
            device_id={"tr": peer}, device_id_type=MESH)

    def ag_copy(k, d):
        peer = lax.rem(me + d + 1, n)
        slot = lax.rem(me, owners)
        return peer, pltpu.make_async_remote_copy(
            src_ref=slabs.at[k, slot], dst_ref=slabs.at[k, slot],
            send_sem=ag_send.at[k, d], recv_sem=ag_recv.at[k, slot],
            device_id={"tr": peer}, device_id_type=MESH)

    def ag_in(k, peer):
        slot = lax.rem(peer, owners)
        return pltpu.make_async_remote_copy(
            src_ref=slabs.at[k, slot], dst_ref=slabs.at[k, slot],
            send_sem=ag_send.at[k, 0], recv_sem=ag_recv.at[k, slot],
            device_id={"tr": peer}, device_id_type=MESH)

    def only(test, body):
        if owners == n:
            body()
        else:
            pl.when(test)(body)

    for k in range(PASSES):
        total = jnp.zeros((rows, spans), jnp.float32)
        for b in range(blocks):
            total += lax.dot_general(
                work[:, block(b)].astype(jnp.bfloat16), sub_v[:, block(b)],
                (((1,), (1,)), ((), ())), preferred_element_type=jnp.float32)
        partial[k] = total

        def send_partial(d):
            peer, copy = rs_copy(k, d)
            only(peer < owners, copy.start)

        each(n - 1, send_partial)

        def own_sum():
            inbox[k, me] = partial[k, rows_of(lax.rem(me, owners))]

            def arrive(d):
                rs_in(k, d)[1].wait_recv()

            each(n - 1, arrive)
            slabs[k, lax.rem(me, owners)] = jnp.sum(inbox[k], axis=0).astype(jnp.bfloat16)

            def spread(d):
                ag_copy(k, d)[1].start()

            each(n - 1, spread)

        only(me < owners, own_sum)

        def gather(d):
            peer = lax.rem(me + d + 1, n)
            only(peer < owners, lambda: ag_in(k, peer).wait_recv())

        each(n - 1, gather)
        coef = jnp.concatenate(
            [slabs[k, j].astype(jnp.float32) for j in range(owners)], axis=0).astype(jnp.bfloat16)
        for b in range(blocks):
            work[:, block(b)] -= jnp.dot(coef, sub_v[:, block(b)], preferred_element_type=jnp.float32)
            if k == PASSES - 1:
                pltpu.make_async_copy(work.at[:, block(b)], out.at[:, block(b)], out_sem.at[b]).start()

    for o in range(1, OFFS):
        part_copy(o).wait_send()
        for d in range(1, roots):
            swap_copy(o, d).wait_send()
    for k in range(PASSES):

        def drain(d):
            peer, copy = rs_copy(k, d)
            only(peer < owners, copy.wait_send)
            only(me < owners, ag_copy(k, d)[1].wait_send)

        each(n - 1, drain)
    for b in range(blocks):
        pltpu.make_async_copy(work.at[:, block(b)], out.at[:, block(b)], out_sem.at[b]).wait()


def per_device(n, roots, residual, subspace, inverses, owner_offset, listed):
    rows, cols = residual.shape
    spans = subspace.shape[0]
    blk = inverses.shape[1]
    blocks = cols // blk
    owners = min(n, rows // SUBLANES)
    slab = rows // owners
    hbm = pl.BlockSpec(memory_space=pl.ANY)
    smem = pl.BlockSpec(memory_space=pltpu.SMEM)
    dma = pltpu.SemaphoreType.DMA
    return pl.pallas_call(
        functools.partial(kernel, n, roots),
        out_shape=jax.ShapeDtypeStruct((rows, cols), jnp.float32),
        in_specs=[smem, smem, hbm, hbm, hbm],
        out_specs=hbm,
        scratch_shapes=[
            pltpu.VMEM((OFFS, blk, blk), jnp.bfloat16),
            pltpu.VMEM((rows, cols), jnp.bfloat16),
            pltpu.VMEM((spans, cols), jnp.bfloat16),
            pltpu.VMEM((rows, cols), jnp.float32),
            pltpu.VMEM((blocks * rows, blk), jnp.bfloat16),
            pltpu.VMEM((PASSES, rows, spans), jnp.float32),
            pltpu.VMEM((PASSES, n, slab, spans), jnp.float32),
            pltpu.VMEM((PASSES, owners, slab, spans), jnp.bfloat16),
            dma((3,)),
            dma((OFFS,)), dma((OFFS,)),
            dma((OFFS, roots)), dma((OFFS, roots)),
            dma((PASSES, n)), dma((PASSES, n)),
            dma((PASSES, n)), dma((PASSES, owners)),
            dma((blocks,)),
        ],
        compiler_params=pltpu.CompilerParams(collective_id=0, has_side_effects=True),
    )(owner_offset, listed, residual, subspace, inverses)


def solution(mesh):
    body = functools.partial(per_device, mesh.shape["tr"], mesh.shape["root"])
    return jax.shard_map(
        body,
        mesh=mesh,
        in_specs=(
            P("root", ("grp", "tr")),
            P(None, ("grp", "tr")),
            P(("grp", "tr"), None, None),
            P(("grp", "tr")),
            P(("grp", "tr")),
        ),
        out_specs=P("root", ("grp", "tr")),
        check_vma=False,
    )
```

time: 140 us -> 60.5 us (0.43)
  blocking collectives: 84.5 us -> 0 us
  Pallas kernels: 0 us -> 58.1 us
  waiting for transfers between devices: 32.9 us -> 0 us
  matrix products: 14 us -> 0 us
  starting transfers between devices: 6.46 us -> 0 us
  other arithmetic: 1.96 us -> 0 us
  local copies, waits for them, and re-layouts: 0.34 us -> 2.27 us
    psum x2 -> x0, blocking collectives: 84.5 us -> none  [per_device(): correlation = lax.psum(partial_correlation, 'tr')]
    pallas_call x0 -> x1, Pallas kernels: none -> 58.1 us  [per_device(): pl.pallas_call(functools.partial(kernel, n, roots), out_shape=jax.ShapeDt...]
    ppermute x3 -> x0, waiting for transfers between devices: 32.9 us -> none  [from_behind(): return lax.ppermute(block, axis, route)]
    dot_general x6 -> x0, matrix products: 14 us -> none  [the longest x2 7.19 us: per_device(): jnp.dot(coefficients, subspace, preferred_element_type=jnp.float32)]
    ppermute x3 -> x0, starting transfers between devices: 6.46 us -> none  [from_behind(): return lax.ppermute(block, axis, route)]
    unnamed x8 -> x1, local copies, waits for them, and re-layouts: 0.27 us -> 2.27 us
  transfers between devices with their start and end apart: 3 -> 0, of which waited for: 3 -> 0; matrix products, arithmetic and copies ran while one was open for 0% -> 0% of each run, Pallas kernels for 0% -> 0%
where the time goes in v1:
time: 60.5 us; the launch traced here: 60.4 us
  Pallas kernels  58.1 us (96%)
  local copies, waits for them, and re-layouts  2.27 us (4%)
    pallas_call x1, Pallas kernels, per_device(): pl.pallas_call(functools.partial(kernel, n, roots), out_shape=jax.ShapeDt...  58.1 us
    unnamed x1, local copies, waits for them, and re-layouts  2.27 us

profile of v1, /device:TPU:0, one launch (start us, length us, event | category | flops | bytes accessed | tf_op | source)
XLA Modules:
  0.0 60.4 jit_solution(7320013455482070049)
XLA Ops:
  0.0 58.1 %shard_map.55 = f32[64,4096]{1,0:T(8,128)} custom-call(s32[8]{0:T(128)} %off.1, s32[8]{0:T(128)} %listed.1, bf16[64,4096]{1,0:T(8,128)(2,1)} %res.1, bf16[512,4096]{1,0:T(8,128)(2,1)} %sub.1, bf16[1,512,512]{2,1,0:T(8,128)(2,1)} %inv.1), custom_call_target="tpu_custom_call" | custom-call | tf_op jit(solution)/shard_map/pallas_call | solution.py:211
  58.1 2.3 %copy.7 = f32[64,4096]{1,0:T(8,128)} copy(f32[64,4096]{1,0:T(8,128)} %shard_map.55) | data formatting | bytes 2097152

commit v2 on v1

--- a/solution.py
+++ b/solution.py
@@ -9,6 +9,8 @@
 OFFS = 4
 PASSES = 2
 SUBLANES = 8
+CHUNKS = 2
+HOPS = 6
 MESH = pl.DeviceIdType.MESH
 
 
@@ -21,7 +23,7 @@
 
 
 def kernel(n, roots, off, listed, res, sub, inv, out, table, res_v, sub_v, work, picked,
-           partial, inbox, slabs, load_sem, part_send, part_recv, swap_send, swap_recv,
+           partial, inbox, slabs, load_sem, hop_send, hop_recv, swap_send, swap_recv,
            rs_send, rs_recv, ag_send, ag_recv, out_sem):
     me = lax.axis_index("tr")
     root = lax.axis_index("root")
@@ -32,12 +34,11 @@
     share = blk // roots
     owners = slabs.shape[1]
     slab = rows // owners
-    mine = pl.ds(pl.multiple_of(root * share, share), share)
 
     def block(b):
         return pl.ds(b * blk, blk)
 
-    own_load = pltpu.make_async_copy(inv.at[0], table.at[0], load_sem.at[0])
+    own_load = pltpu.make_async_copy(inv.at[0], table.at[lax.rem(me, 2)], load_sem.at[0])
     own_load.start()
     res_load = pltpu.make_async_copy(res, res_v, load_sem.at[1])
     res_load.start()
@@ -54,28 +55,77 @@
         pl.semaphore_signal(barrier, inc=1, device_id={"root": lax.rem(root + d, roots)}, device_id_type=MESH)
     pl.semaphore_wait(barrier, n - 1 + roots - 1)
 
-    def part_copy(o):
+    side = lax.rem(me, 2)
+    chunk = share // CHUNKS
+
+    def chunk_rows(half, q):
+        return pl.ds(pl.multiple_of(half * share + q * chunk, chunk), chunk)
+
+    def hop(src, q, slot, peer, sem):
         return pltpu.make_async_remote_copy(
-            src_ref=inv.at[0, mine], dst_ref=table.at[o, mine],
-            send_sem=part_send.at[o], recv_sem=part_recv.at[o],
-            device_id={"tr": lax.rem(me + n - o, n)}, device_id_type=MESH)
-
-    def swap_copy(o, d):
+            src_ref=src, dst_ref=table.at[slot, chunk_rows(root, q)],
+            send_sem=hop_send.at[sem, q], recv_sem=hop_recv.at[slot, q],
+            device_id={"tr": lax.rem(peer + n, n)}, device_id_type=MESH)
+
+    def own_hop(q, slot, peer, sem):
+        return hop(inv.at[0, chunk_rows(root, q)], q, slot, peer, sem)
+
+    def relay(e, q, slot, peer, sem):
+        return hop(table.at[e, chunk_rows(root, q)], q, slot, peer, sem)
+
+    def swap(e, q, half):
+        rows_q = table.at[e, chunk_rows(half, q)]
         return pltpu.make_async_remote_copy(
-            src_ref=table.at[o, mine], dst_ref=table.at[o, mine],
-            send_sem=swap_send.at[o, d], recv_sem=swap_recv.at[o, d],
-            device_id={"root": lax.rem(root + d, roots)}, device_id_type=MESH)
-
-    def swap_in(o, d):
-        other = lax.rem(root + roots - d, roots)
-        theirs = pl.ds(pl.multiple_of(other * share, share), share)
-        return pltpu.make_async_remote_copy(
-            src_ref=table.at[o, theirs], dst_ref=table.at[o, theirs],
-            send_sem=swap_send.at[o, d], recv_sem=swap_recv.at[o, d],
-            device_id={"root": other}, device_id_type=MESH)
-
-    for o in range(1, OFFS):
-        part_copy(o).start()
+            src_ref=rows_q, dst_ref=rows_q,
+            send_sem=swap_send.at[e, q], recv_sem=swap_recv.at[e, q],
+            device_id={"root": 1 - root}, device_id_type=MESH)
+
+    twin = me + 1 - 2 * side
+    near = me - 2
+    far = me - 4
+    roles = {
+        (0, 0): ([(2, near), (4, far)], [(1, [(3, near)]), (2, [(2, twin)]), (4, [(4, twin)]), (3, [(3, twin)])]),
+        (1, 1): ([(3, near), (1, twin)], [(0, [(2, near), (4, far)]), (3, [(3, twin)]), (2, [(2, twin)]), (4, [])]),
+        (1, 0): ([(1, twin)], [(2, []), (4, []), (3, [])]),
+        (0, 1): ([(0, twin)], [(1, []), (3, []), (2, [])]),
+    }
+
+    def per_role(body):
+        for (s, r), (own, events) in roles.items():
+            pl.when(jnp.logical_and(side == s, root == r))(functools.partial(body, s, own, events))
+
+    def sem_of(events, i, j):
+        return 2 + sum(len(targets) for _, targets in events[:i]) + j
+
+    def open_hops(s, own, events):
+        for j, (slot, peer) in enumerate(own):
+            for q in range(CHUNKS):
+                own_hop(q, slot, peer, j).start()
+
+    def run_events(first, s, own, events):
+        cut = len(events) - 1
+        for i, (e, targets) in enumerate(events):
+            if (i < cut) != first:
+                continue
+            for q in range(CHUNKS):
+                relay(e, q, e, twin, 0).wait_recv()
+                for j, (slot, peer) in enumerate(targets):
+                    relay(e, q, slot, peer, sem_of(events, i, j)).start()
+                if s < e < s + OFFS:
+                    swap(e, q, root).start()
+
+    def close_hops(s, own, events):
+        for j, (slot, peer) in enumerate(own):
+            for q in range(CHUNKS):
+                own_hop(q, slot, peer, j).wait_send()
+        for i, (e, targets) in enumerate(events):
+            for q in range(CHUNKS):
+                for j, (slot, peer) in enumerate(targets):
+                    relay(e, q, slot, peer, sem_of(events, i, j)).wait_send()
+                if s < e < s + OFFS:
+                    swap(e, q, root).wait_send()
+
+    per_role(open_hops)
 
     res_load.wait()
     for b in range(blocks):
@@ -88,18 +138,21 @@
             x = res_v[:, block(b)].astype(jnp.float32)
             picked[pl.ds(b * rows, rows), :] = jnp.where(hit, x, 0.0).astype(jnp.bfloat16)
         for b in range(blocks):
-            part = jnp.dot(picked[pl.ds(b * rows, rows), :], table[o], preferred_element_type=jnp.float32)
+            part = jnp.dot(picked[pl.ds(b * rows, rows), :], table[side + o], preferred_element_type=jnp.float32)
             work[:, block(b)] += part
+
+    def arrive_and_apply(o):
+        for q in range(CHUNKS):
+            swap(side + o, q, 1 - root).wait_recv()
+        apply(o)
 
     own_load.wait()
     apply(0)
-    for o in range(1, OFFS):
-        part_copy(o).wait_recv()
-        for d in range(1, roots):
-            swap_copy(o, d).start()
-        for d in range(1, roots):
-            swap_in(o, d).wait_recv()
-        apply(o)
+    per_role(functools.partial(run_events, True))
+    arrive_and_apply(1)
+    per_role(functools.partial(run_events, False))
+    for o in range(2, OFFS):
+        arrive_and_apply(o)
     sub_load.wait()
 
     def rows_of(j):
@@ -182,10 +235,7 @@
             if k == PASSES - 1:
                 pltpu.make_async_copy(work.at[:, block(b)], out.at[:, block(b)], out_sem.at[b]).start()
 
-    for o in range(1, OFFS):
-        part_copy(o).wait_send()
-        for d in range(1, roots):
-            swap_copy(o, d).wait_send()
+    per_role(close_hops)
     for k in range(PASSES):
 
         def drain(d):
@@ -214,7 +264,7 @@
         in_specs=[smem, smem, hbm, hbm, hbm],
         out_specs=hbm,
         scratch_shapes=[
-            pltpu.VMEM((OFFS, blk, blk), jnp.bfloat16),
+            pltpu.VMEM((OFFS + 1, blk, blk), jnp.bfloat16),
             pltpu.VMEM((rows, cols), jnp.bfloat16),
             pltpu.VMEM((spans, cols), jnp.bfloat16),
             pltpu.VMEM((rows, cols), jnp.float32),
@@ -223,8 +273,8 @@
             pltpu.VMEM((PASSES, n, slab, spans), jnp.float32),
             pltpu.VMEM((PASSES, owners, slab, spans), jnp.bfloat16),
             dma((3,)),
-            dma((OFFS,)), dma((OFFS,)),
-            dma((OFFS, roots)), dma((OFFS, roots)),
+            dma((HOPS, CHUNKS)), dma((OFFS + 1, CHUNKS)),
+            dma((OFFS + 1, CHUNKS)), dma((OFFS + 1, CHUNKS)),
             dma((PASSES, n)), dma((PASSES, n)),
             dma((PASSES, n)), dma((PASSES, owners)),
             dma((blocks,)),

time: 60.5 us -> 55.3 us (0.914)
  Pallas kernels: 58.1 us -> 52.9 us
    pallas_call x1, Pallas kernels: 58.1 us -> 52.9 us  [per_device(): pl.pallas_call(functools.partial(kernel, n, roots), out_shape=jax.ShapeDt...]
where the time goes in v2:
time: 55.3 us; the launch traced here: 55.1 us
  Pallas kernels  52.9 us (96%)
  local copies, waits for them, and re-layouts  2.27 us (4%)
    pallas_call x1, Pallas kernels, per_device(): pl.pallas_call(functools.partial(kernel, n, roots), out_shape=jax.ShapeDt...  52.9 us
    unnamed x1, local copies, waits for them, and re-layouts  2.27 us

profile of v2, /device:TPU:0, one launch (start us, length us, event | category | flops | bytes accessed | tf_op | source)
XLA Modules:
  0.0 55.1 jit_solution(18358104588125635545)
XLA Ops:
  0.0 52.9 %shard_map.55 = f32[64,4096]{1,0:T(8,128)} custom-call(s32[8]{0:T(128)} %off.1, s32[8]{0:T(128)} %listed.1, bf16[64,4096]{1,0:T(8,128)(2,1)} %res.1, bf16[512,4096]{1,0:T(8,128)(2,1)} %sub.1, bf16[1,512,512]{2,1,0:T(8,128)(2,1)} %inv.1), custom_call_target="tpu_custom_call" | custom-call | tf_op jit(solution)/shard_map/pallas_call | solution.py:261
  52.9 2.3 %copy.7 = f32[64,4096]{1,0:T(8,128)} copy(f32[64,4096]{1,0:T(8,128)} %shard_map.55) | data formatting | bytes 2097152

commit v3 on v2

v3 whole, which is shorter than its diff:
```python
import functools
import jax
import jax.numpy as jnp
from jax import lax
from jax.experimental import pallas as pl
from jax.experimental.pallas import tpu as pltpu
from jax.sharding import PartitionSpec as P

OFFS = 4
PASSES = 2
PARTS = 1
LINK = jnp.bfloat16
SUBLANES = 8
CHUNKS = 4
HOPS = 6
MESH = pl.DeviceIdType.MESH


def each(count, body):
    if count <= 16:
        for i in range(count):
            body(i)
    else:
        pl.loop(0, count)(body)


def kernel(n, roots, off, listed, res, sub, inv, out, table, res_v, sub_v, work, picked,
           partial, inbox, slabs, load_sem, hop_send, hop_recv, swap_send, swap_recv,
           rs_send, rs_recv, ag_send, ag_recv, out_sem):
    me = lax.axis_index("tr")
    root = lax.axis_index("root")
    rows, cols = res.shape
    blk = inv.shape[1]
    blocks = cols // blk
    width = sub.shape[0] // PARTS
    share = blk // roots
    owners = slabs.shape[1]
    base = (n - owners) // 2
    slab = rows // owners

    def block(b):
        return pl.ds(b * blk, blk)

    own_load = pltpu.make_async_copy(inv.at[0], table.at[lax.rem(me, 2)], load_sem.at[0])
    own_load.start()
    res_load = pltpu.make_async_copy(res, res_v, load_sem.at[1])
    res_load.start()
    sub_load = pltpu.make_async_copy(sub, sub_v, load_sem.at[2])
    sub_load.start()

    barrier = pltpu.get_barrier_semaphore()

    def is_owner(device):
        return jnp.logical_and(device >= base, device < base + owners)

    side = lax.rem(me, 2)
    twin = me + 1 - 2 * side

    def linked(d):
        peer = lax.rem(me + d + 1, n)
        close = jnp.logical_or(jnp.logical_or(d + 1 == 2, d + 1 == n - 2), peer == twin)
        return jnp.logical_or(close, jnp.logical_or(is_owner(me), is_owner(peer)))

    def greet(d):
        def signal():
            pl.semaphore_signal(barrier, inc=1, device_id={"tr": lax.rem(me + d + 1, n)}, device_id_type=MESH)

        pl.when(linked(d))(signal)

    each(n - 1, greet)
    for d in range(1, roots):
        pl.semaphore_signal(barrier, inc=1, device_id={"root": lax.rem(root + d, roots)}, device_id_type=MESH)
    partners = lax.fori_loop(0, n - 1, lambda d, c: c + linked(d).astype(jnp.int32), jnp.int32(roots - 1))
    pl.semaphore_wait(barrier, partners)

    chunk = share // CHUNKS

    def chunk_rows(half, q):
        return pl.ds(pl.multiple_of(half * share + q * chunk, chunk), chunk)

    def hop(src, q, slot, peer, sem):
        return pltpu.make_async_remote_copy(
            src_ref=src, dst_ref=table.at[slot, chunk_rows(root, q)],
            send_sem=hop_send.at[sem, q], recv_sem=hop_recv.at[slot, q],
            device_id={"tr": lax.rem(peer + n, n)}, device_id_type=MESH)

    def own_hop(q, slot, peer, sem):
        return hop(inv.at[0, chunk_rows(root, q)], q, slot, peer, sem)

    def relay(e, q, slot, peer, sem):
        return hop(table.at[e, chunk_rows(root, q)], q, slot, peer, sem)

    def swap(e, q, half):
        rows_q = table.at[e, chunk_rows(half, q)]
        return pltpu.make_async_remote_copy(
            src_ref=rows_q, dst_ref=rows_q,
            send_sem=swap_send.at[e, q], recv_sem=swap_recv.at[e, q],
            device_id={"root": 1 - root}, device_id_type=MESH)

    near = me - 2
    roles = {
        (0, 0): ([(2, near)], [(1, [(3, near)], []), (2, [(4, near), (2, twin)], []), (3, [(3, twin)], []), (4, [(4, twin)], [])]),
        (1, 1): ([(3, near)], [(0, [(2, near)], [(1, twin)]), (3, [(3, twin)], []), (2, [(4, near), (2, twin)], []), (4, [], [])]),
        (1, 0): ([(1, twin)], [(2, [], []), (3, [], []), (4, [], [])]),
        (0, 1): ([(0, twin)], [(1, [], []), (3, [], []), (2, [], [])]),
    }

    def per_role(body):
        for (s, r), (own, events) in roles.items():
            pl.when(jnp.logical_and(side == s, root == r))(functools.partial(body, s, own, events))

    def sem_of(events, i, j):
        return 1 + sum(len(targets) + len(late) for _, targets, late in events[:i]) + j

    def open_hops(s, own, events):
        for j, (slot, peer) in enumerate(own):
            for q in range(CHUNKS):
                own_hop(q, slot, peer, j).start()

    def run_events(first, s, own, events):
        cut = len(events) - 1
        for i, (e, targets, late) in enumerate(events):
            if (i < cut) != first:
                continue
            for q in range(CHUNKS):
                relay(e, q, e, twin, 0).wait_recv()
                for j, (slot, peer) in enumerate(targets):
                    relay(e, q, slot, peer, sem_of(events, i, j)).start()
                for j, (slot, peer) in enumerate(late):
                    own_hop(q, slot, peer, sem_of(events, i, len(targets) + j)).start()
                if s < e < s + OFFS:
                    swap(e, q, root).start()

    def close_hops(s, own, events):
        for j, (slot, peer) in enumerate(own):
            for q in range(CHUNKS):
                own_hop(q, slot, peer, j).wait_send()
        for i, (e, targets, late) in enumerate(events):
            for q in range(CHUNKS):
                for j, (slot, peer) in enumerate(targets):
                    relay(e, q, slot, peer, sem_of(events, i, j)).wait_send()
                for j, (slot, peer) in enumerate(late):
                    own_hop(q, slot, peer, sem_of(events, i, len(targets) + j)).wait_send()
                if s < e < s + OFFS:
                    swap(e, q, root).wait_send()

    per_role(open_hops)

    res_load.wait()
    for b in range(blocks):
        kept = jnp.where(listed[b] > 0, 0.0, res_v[:, block(b)].astype(jnp.float32))
        work[:, block(b)] = kept

    def apply(o):
        for b in range(blocks):
            hit = jnp.logical_and(listed[b] > 0, off[b] == o)
            x = res_v[:, block(b)].astype(jnp.float32)
            picked[pl.ds(b * rows, rows), :] = jnp.where(hit, x, 0.0).astype(jnp.bfloat16)
        for b in range(blocks):
            part = jnp.dot(picked[pl.ds(b * rows, rows), :], table[side + o], preferred_element_type=jnp.float32)
            work[:, block(b)] += part

    def arrive_and_apply(o):
        for q in range(CHUNKS):
            swap(side + o, q, 1 - root).wait_recv()
        apply(o)

    own_load.wait()
    apply(0)
    per_role(functools.partial(run_events, True))
    arrive_and_apply(1)
    per_role(functools.partial(run_events, False))
    for o in range(2, OFFS):
        arrive_and_apply(o)
    sub_load.wait()

    def rs_copy(i, j):
        return pltpu.make_async_remote_copy(
            src_ref=partial.at[i, j], dst_ref=inbox.at[i, me],
            send_sem=rs_send.at[i, j], recv_sem=rs_recv.at[i, me],
            device_id={"tr": base + j}, device_id_type=MESH)

    def rs_in(i, peer):
        return pltpu.make_async_remote_copy(
            src_ref=inbox.at[i, peer], dst_ref=inbox.at[i, peer],
            send_sem=rs_send.at[i, 0], recv_sem=rs_recv.at[i, peer],
            device_id={"tr": peer}, device_id_type=MESH)

    def ag_copy(i, d):
        return pltpu.make_async_remote_copy(
            src_ref=slabs.at[i, me - base], dst_ref=slabs.at[i, me - base],
            send_sem=ag_send.at[i, d], recv_sem=ag_recv.at[i, me - base],
            device_id={"tr": lax.rem(me + d + 1, n)}, device_id_type=MESH)

    def ag_in(i, j):
        return pltpu.make_async_remote_copy(
            src_ref=slabs.at[i, j], dst_ref=slabs.at[i, j],
            send_sem=ag_send.at[i, 0], recv_sem=ag_recv.at[i, j],
            device_id={"tr": base + j}, device_id_type=MESH)

    def span(h):
        return pl.ds(h * width, width)

    def for_other_owners(body):
        for j in range(owners):
            pl.when(me != base + j)(functools.partial(body, j))

    for k in range(PASSES):
        for b in range(blocks):
            res_v[:, block(b)] = work[:, block(b)].astype(jnp.bfloat16)
        for h in range(PARTS):
            i = k * PARTS + h
            total = jnp.zeros((rows, width), jnp.float32)
            for b in range(blocks):
                total += lax.dot_general(
                    res_v[:, block(b)], sub_v[span(h), block(b)],
                    (((1,), (1,)), ((), ())), preferred_element_type=jnp.float32)
            partial[i] = total.reshape(owners, slab, width).astype(partial.dtype)

            for_other_owners(lambda j: rs_copy(i, j).start())

        def own_sum(i):
            inbox[i, me] = partial[i, me - base]
            each(n - 1, lambda d: rs_in(i, lax.rem(me + d + 1, n)).wait_recv())
            slabs[i, me - base] = jnp.sum(inbox[i].astype(jnp.float32), axis=0).astype(jnp.bfloat16)
            each(n - 1, lambda d: ag_copy(i, d).start())

        for h in range(PARTS):
            pl.when(is_owner(me))(functools.partial(own_sum, k * PARTS + h))
        for h in range(PARTS):
            i = k * PARTS + h
            for_other_owners(lambda j: ag_in(i, j).wait_recv())
            coef = jnp.concatenate(
                [slabs[i, j].astype(jnp.float32) for j in range(owners)], axis=0).astype(jnp.bfloat16)
            for b in range(blocks):
                work[:, block(b)] -= jnp.dot(
                    coef, sub_v[span(h), block(b)], preferred_element_type=jnp.float32)
                if i == PASSES * PARTS - 1:
                    pltpu.make_async_copy(work.at[:, block(b)], out.at[:, block(b)], out_sem.at[b]).start()

    per_role(close_hops)
    for i in range(PASSES * PARTS):
        for_other_owners(lambda j: rs_copy(i, j).wait_send())

        def sent():
            each(n - 1, lambda d: ag_copy(i, d).wait_send())

        pl.when(is_owner(me))(sent)
    for b in range(blocks):
        pltpu.make_async_copy(work.at[:, block(b)], out.at[:, block(b)], out_sem.at[b]).wait()


def per_device(n, roots, residual, subspace, inverses, owner_offset, listed):
    rows, cols = residual.shape
    spans = subspace.shape[0]
    blk = inverses.shape[1]
    blocks = cols // blk
    owners = min(n // 2, rows // SUBLANES)
    slab = rows // owners
    rounds = PASSES * PARTS
    hbm = pl.BlockSpec(memory_space=pl.ANY)
    smem = pl.BlockSpec(memory_space=pltpu.SMEM)
    dma = pltpu.SemaphoreType.DMA
    return pl.pallas_call(
        functools.partial(kernel, n, roots),
        out_shape=jax.ShapeDtypeStruct((rows, cols), jnp.float32),
        in_specs=[smem, smem, hbm, hbm, hbm],
        out_specs=hbm,
        scratch_shapes=[
            pltpu.VMEM((OFFS + 1, blk, blk), jnp.bfloat16),
            pltpu.VMEM((rows, cols), jnp.bfloat16),
            pltpu.VMEM((spans, cols), jnp.bfloat16),
            pltpu.VMEM((rows, cols), jnp.float32),
            pltpu.VMEM((blocks * rows, blk), jnp.bfloat16),
            pltpu.VMEM((rounds, owners, slab, spans // PARTS), LINK),
            pltpu.VMEM((rounds, n, slab, spans // PARTS), LINK),
            pltpu.VMEM((rounds, owners, slab, spans // PARTS), jnp.bfloat16),
            dma((3,)),
            dma((HOPS, CHUNKS)), dma((OFFS + 1, CHUNKS)),
            dma((OFFS + 1, CHUNKS)), dma((OFFS + 1, CHUNKS)),
            dma((rounds, owners)), dma((rounds, n)),
            dma((rounds, n)), dma((rounds, owners)),
            dma((blocks,)),
        ],
        compiler_params=pltpu.CompilerParams(collective_id=0, has_side_effects=True),
    )(owner_offset, listed, residual, subspace, inverses)


def solution(mesh):
    body = functools.partial(per_device, mesh.shape["tr"], mesh.shape["root"])
    return jax.shard_map(
        body,
        mesh=mesh,
        in_specs=(
            P("root", ("grp", "tr")),
            P(None, ("grp", "tr")),
            P(("grp", "tr"), None, None),
            P(("grp", "tr")),
            P(("grp", "tr")),
        ),
        out_specs=P("root", ("grp", "tr")),
        check_vma=False,
    )
```

time: 55.3 us -> 50.7 us (0.917)
  Pallas kernels: 52.9 us -> 48.3 us
    pallas_call x1, Pallas kernels: 52.9 us -> 48.3 us  [per_device(): pl.pallas_call(functools.partial(kernel, n, roots), out_shape=jax.ShapeDt...]
where the time goes in v3:
time: 50.7 us; the launch traced here: 50.6 us
  Pallas kernels  48.3 us (95%)
  local copies, waits for them, and re-layouts  2.27 us (4%)
    pallas_call x1, Pallas kernels, per_device(): pl.pallas_call(functools.partial(kernel, n, roots), out_shape=jax.ShapeDt...  48.3 us
    unnamed x1, local copies, waits for them, and re-layouts  2.27 us

profile of v3, /device:TPU:0, one launch (start us, length us, event | category | flops | bytes accessed | tf_op | source)
XLA Modules:
  0.0 50.6 jit_solution(219363588576634057)
XLA Ops:
  0.0 48.3 %shard_map.55 = f32[64,4096]{1,0:T(8,128)} custom-call(s32[8]{0:T(128)} %off.1, s32[8]{0:T(128)} %listed.1, bf16[64,4096]{1,0:T(8,128)(2,1)} %res.1, bf16[512,4096]{1,0:T(8,128)(2,1)} %sub.1, bf16[1,512,512]{2,1,0:T(8,128)(2,1)} %inv.1), custom_call_target="tpu_custom_call" | custom-call | tf_op jit(solution)/shard_map/pallas_call | solution.py:264
  48.3 2.3 %copy.7 = f32[64,4096]{1,0:T(8,128)} copy(f32[64,4096]{1,0:T(8,128)} %shard_map.55) | data formatting | bytes 2097152

commit v4 on v3

--- a/solution.py
+++ b/solution.py
@@ -100,7 +100,7 @@
     near = me - 2
     roles = {
         (0, 0): ([(2, near)], [(1, [(3, near)], []), (2, [(4, near), (2, twin)], []), (3, [(3, twin)], []), (4, [(4, twin)], [])]),
-        (1, 1): ([(3, near)], [(0, [(2, near)], [(1, twin)]), (3, [(3, twin)], []), (2, [(4, near), (2, twin)], []), (4, [], [])]),
+        (1, 1): ([(3, near)], [(0, [(2, near)], []), (3, [(3, twin)], [(1, twin)]), (2, [(4, near), (2, twin)], []), (4, [], [])]),
         (1, 0): ([(1, twin)], [(2, [], []), (3, [], []), (4, [], [])]),
         (0, 1): ([(0, twin)], [(1, [], []), (3, [], []), (2, [], [])]),
     }

time: 50.7 us -> 50.5 us (level)
  no operation moved by 1% of the time
where the time goes in v4:
time: 50.5 us; the launch traced here: 50.4 us
  Pallas kernels  48.1 us (95%)
  local copies, waits for them, and re-layouts  2.27 us (4%)
    pallas_call x1, Pallas kernels, per_device(): pl.pallas_call(functools.partial(kernel, n, roots), out_shape=jax.ShapeDt...  48.1 us
    unnamed x1, local copies, waits for them, and re-layouts  2.27 us

profile of v4, /device:TPU:0, one launch (start us, length us, event | category | flops | bytes accessed | tf_op | source)
XLA Modules:
  0.0 50.4 jit_solution(18101628483119532898)
XLA Ops:
  0.0 48.1 %shard_map.55 = f32[64,4096]{1,0:T(8,128)} custom-call(s32[8]{0:T(128)} %off.1, s32[8]{0:T(128)} %listed.1, bf16[64,4096]{1,0:T(8,128)(2,1)} %res.1, bf16[512,4096]{1,0:T(8,128)(2,1)} %sub.1, bf16[1,512,512]{2,1,0:T(8,128)(2,1)} %inv.1), custom_call_target="tpu_custom_call" | custom-call | tf_op jit(solution)/shard_map/pallas_call | solution.py:264
  48.1 2.3 %copy.7 = f32[64,4096]{1,0:T(8,128)} copy(f32[64,4096]{1,0:T(8,128)} %shard_map.55) | data formatting | bytes 2097152
